TPU v7x, 128 devices: a whole 4x4x4 slice. The times are simulated.
128 devices in a mesh: leaf: 8 (over y_lo, z), front: 16 (over x, y_hi, core).
Axes of the slice: x: 4, y: 4 (y_hi: 2, y_lo: 2; y = y_hi * 2 + y_lo), z: 4, core: 2. Of those that a mesh axis runs over, the one named last changes fastest.
Arguments:
- leaf_fronts: float32 [32768, 4096], P('leaf', 'front'), as said below
- root_front: float32 [4096, 16, 256], P(None, 'front', 'leaf'), as said below
- leaf_order: int32 [8, 16], P('leaf'), may hold values from 0 to 15, each once within a row
- leaf_map: int32 [8, 16], P('leaf'), may hold values from 0 to 15, each once within a row
- root_order: int32 [16], replicated, may hold values from 0 to 15, each once
Outputs:
- leaf_factor: float32 [32768, 4096], P('leaf', 'front')
- root_factor: float32 [4096, 16, 256], P(None, 'front', 'leaf')
Inputs may be any that keep to these rules, and one draw needn't show every extreme that they name: `leaf_fronts`: each leaf block of 4096 rows is symmetric and positive definite. `root_front`: symmetric and positive definite. `leaf_order`: each row names every block column once. `leaf_map`: each row names every root block once. `root_order`: names every block column once.
All inputs are finite; a program needn't handle non-finite values.
Results may differ from a plain program's by a relative error of at most 0.00018.
Values sent between devices are 32-bit elements; how exact they have to be, the bound alone decides.
A program may use at most 128 MiB of HBM per device.

v0:
```python
import jax
import jax.numpy as jnp
from jax import lax
from jax.sharding import PartitionSpec as P

HIGH = lax.Precision.HIGH


def invert(permutation):
    block_ids = jnp.arange(permutation.shape[0], dtype=jnp.int32)
    hits = permutation[None, :] == block_ids[:, None]
    return jnp.sum(jnp.where(hits, block_ids[None, :], 0), axis=1)


def make_panel(raw_column, pivot_block, alive_set):
    block_size = raw_column.shape[1]
    block_count = raw_column.shape[0] // block_size
    diag_block = lax.dynamic_slice_in_dim(raw_column, pivot_block * block_size, block_size, 0)
    lower = jnp.linalg.cholesky(diag_block)
    solved = lax.linalg.triangular_solve(
        lower, raw_column, left_side=False, lower=True, transpose_a=True
    )
    block_ids = jnp.arange(block_count, dtype=jnp.int32)
    keep = (alive_set & (block_ids != pivot_block))[:, None, None]
    tiles = solved.reshape(block_count, block_size, block_size)
    on_pivot = (block_ids == pivot_block)[:, None, None]
    tiles = jnp.where(on_pivot, lower[None], jnp.where(keep, tiles, 0.0))
    return tiles.reshape(block_count * block_size, block_size)


def block_row(tiles, pivot_block):
    return lax.dynamic_index_in_dim(tiles, pivot_block, 0, keepdims=False)


def shards(leaf_fronts, root_front, leaf_order, leaf_map, root_order):
    order_rows, block_size = leaf_fronts.shape
    block_count = order_rows // block_size
    my_block = lax.axis_index("front")
    leaf_index = lax.axis_index("leaf")
    slice_width = root_front.shape[2]
    block_ids = jnp.arange(block_count, dtype=jnp.int32)
    own_start = my_block * block_size
    tiles = leaf_fronts.reshape(block_count, block_size, block_size)
    first, second = (leaf_order[0, 0], leaf_order[0, 1])
    raw_first = lax.all_gather(block_row(tiles, first).T, "front", axis=0, tiled=True)
    raw_second = lax.all_gather(block_row(tiles, second).T, "front", axis=0, tiled=True)
    everything = jnp.ones((block_count,), dtype=jnp.bool_)
    panel_first = make_panel(raw_first, first, everything)
    alive = block_ids != first
    pivot_rows = lax.dynamic_slice_in_dim(panel_first, second * block_size, block_size, 0)
    raw_second = raw_second - jnp.dot(panel_first, pivot_rows.T, precision=HIGH)
    panel_second = make_panel(raw_second, second, alive)
    alive = alive & (block_ids != second)
    own_first = lax.dynamic_slice_in_dim(panel_first, own_start, block_size, 0)
    own_second = lax.dynamic_slice_in_dim(panel_second, own_start, block_size, 0)
    updated = (
        leaf_fronts
        - jnp.dot(panel_first, own_first.T, precision=HIGH)
        - jnp.dot(panel_second, own_second.T, precision=HIGH)
    )
    updated = updated.reshape(block_count, block_size, block_size)
    updated = jnp.where(alive[:, None, None], updated, 0.0)
    leaf_out = jnp.where(
        my_block == first,
        panel_first,
        jnp.where(my_block == second, panel_second, updated.reshape(order_rows, block_size)),
    )
    mine_alive = alive[my_block]
    inverse = invert(leaf_map[0])
    outgoing = jnp.take(jnp.where(mine_alive, updated, 0.0), inverse, axis=0)
    incoming = lax.all_to_all(outgoing, "front", split_axis=0, concat_axis=0, tiled=True)
    gathered = jnp.swapaxes(jnp.take(incoming, inverse, axis=0), 0, 1)
    gathered = gathered.reshape(block_size, order_rows)
    part = lax.psum_scatter(gathered, "leaf", scatter_dimension=0, tiled=True)
    part = part + root_front[:, 0, :].T
    pivot = root_order[0]
    row = lax.dynamic_slice_in_dim(part, pivot * block_size, block_size, 1)
    raw_root = lax.all_gather(row, ("front", "leaf"), axis=0, tiled=True)
    panel = make_panel(raw_root, pivot, everything)
    own = lax.dynamic_slice_in_dim(panel, own_start + leaf_index * slice_width, slice_width, 0)
    part = part - jnp.dot(own, panel.T, precision=HIGH)
    part = part.reshape(slice_width, block_count, block_size)
    part = jnp.where((block_ids != pivot)[None, :, None], part, 0.0)
    part = part.reshape(slice_width, order_rows)
    own_panel = lax.dynamic_slice_in_dim(panel, leaf_index * slice_width, slice_width, 1)
    root_out = jnp.where(my_block == pivot, own_panel, part.T)
    return (leaf_out, root_out[:, None, :])


def solution(mesh):
    return jax.shard_map(
        shards,
        mesh=mesh,
        in_specs=(
            P("leaf", "front"),
            P(None, "front", "leaf"),
            P("leaf", None),
            P("leaf", None),
            P(),
        ),
        out_specs=(P("leaf", "front"), P(None, "front", "leaf")),
        check_vma=False,
    )
```

profile of v0, /device:TPU:1, one launch (start us, length us, event | category | flops | bytes accessed | tf_op | source)
XLA Modules:
  0.0 781.4 jit_solution(6167048104012507612)
XLA Ops:
  11.8 1.9 dynamic-slice_bitcast_fusion
  16.7 5.6 copy.75
  25.0 51.5 %all-gather.4.cloned.1.call-done = f32[4096,256]{0,1:T(8,128)} async-done(((f32[256,256]{0,1:T(8,128)}), f32[4096,256]{0,1:T(8,128)}) %all-gather.4.cloned.1.call-update) | async-done | bytes 4194320 | tf_op jit(solution)/shard_map/all_gather | solution.py:45
  78.7 11.7 %cholesky.172 = f32[128,128]{1,0:T(8,128)S(1)} custom-call(f32[128,128]{1,0:T(8,128)S(1)} %cholesky.270), custom_call_target="Cholesky" | custom-call | tf_op jit(solution)/shard_map/jit(cholesky)/cholesky | solution.py:19
  90.4 9.8 %custom-call.15 = f32[1,128,128]{1,2,0:T(8,128)S(1)} custom-call(f32[1,128,128]{2,1,0:T(8,128)S(1)} %get-tuple-element.87), custom_call_target="InvertDiagBlocksLowerTriangular" | custom-call | tf_op jit(solution)/shard_map/jit(cholesky)/cholesky | solution.py:19
  100.7 11.7 %cholesky.189 = f32[128,128]{1,0:T(8,128)S(1)} custom-call(f32[128,128]{1,0:T(8,128)S(1)} %convolution_subtract_fusion.9), custom_call_target="Cholesky" | custom-call | tf_op jit(solution)/shard_map/jit(cholesky)/cholesky | solution.py:19
  114.6 3.8 while.6
  118.4 20.0 %custom-call.16 = f32[2,128,128]{1,2,0:T(8,128)S(1)} custom-call(f32[2,128,128]{2,1,0:T(8,128)S(1)} %get-tuple-element.25), custom_call_target="InvertDiagBlocksLowerTriangular" | custom-call | tf_op jit(solution)/shard_map/triangular_solve/custom-call.0 | solution.py:20
  138.8 3.9 copy.94
  142.6 1.9 fusion.11
  144.6 2.1 convolution_subtract_fusion.5
  146.6 2.0 fusion.31
  148.6 2.8 fusion.4
  151.5 5.7 convolution_subtract_fusion.2
  157.2 2.0 copy-done.1
  160.3 11.7 %cholesky.206 = f32[128,128]{1,0:T(8,128)S(1)} custom-call(f32[128,128]{1,0:T(8,128)S(1)} %cholesky.273), custom_call_target="Cholesky" | custom-call | tf_op jit(solution)/shard_map/jit(cholesky)/cholesky | solution.py:19
  172.7 9.8 %custom-call.17 = f32[1,128,128]{1,2,0:T(8,128)S(1)} custom-call(f32[1,128,128]{2,1,0:T(8,128)S(1)} %get-tuple-element.83), custom_call_target="InvertDiagBlocksLowerTriangular" | custom-call | tf_op jit(solution)/shard_map/jit(cholesky)/cholesky | solution.py:19
  183.0 11.7 %cholesky.223 = f32[128,128]{1,0:T(8,128)S(1)} custom-call(f32[128,128]{1,0:T(8,128)S(1)} %convolution_subtract_fusion.8), custom_call_target="Cholesky" | custom-call | tf_op jit(solution)/shard_map/jit(cholesky)/cholesky | solution.py:19
  197.0 4.1 while.7
  201.1 20.1 %custom-call.18 = f32[2,128,128]{1,2,0:T(8,128)S(1)} custom-call(f32[2,128,128]{2,1,0:T(8,128)S(1)} %get-tuple-element.26), custom_call_target="InvertDiagBlocksLowerTriangular" | custom-call | tf_op jit(solution)/shard_map/triangular_solve/custom-call.0 | solution.py:20
  221.2 3.6 fusion.9
  224.8 2.0 convolution_subtract_fusion.4
  226.8 2.0 fusion.27
  229.2 3.9 copy.95
  233.1 2.2 convolution_subtract_fusion.1
  236.1 6.2 select_select_fusion.1
  242.3 5.6 copy.90
  247.9 5.3 select_select_fusion
  253.2 4.9 gather_fusion
  258.1 2.8 broadcast_select_fusion
  260.9 54.1 %all_to_all.5 = f32[16,256,256]{2,1,0:T(8,128)} all-to-all(f32[16,256,256]{2,1,0:T(8,128)S(1)} %broadcast_select_fusion), channel_id=1, replica_groups=mesh['leaf'=8,'front'=16] {'front'}, dimensions={0} | all-to-all | bytes 8388608 | tf_op jit(solution)/shard_map/all_to_all | solution.py:71
  315.1 5.0 gather_fusion.1
  320.1 4.7 select_bitcast_fusion
  324.8 5.3 copy.79
  330.1 5.6 copy.91
  336.4 51.2 %reduce-scatter.4.cloned.1.call-done = f32[32,4096]{1,0:T(8,128)} async-done(((f32[256,4096]{1,0:T(8,128)}), f32[32,4096]{1,0:T(8,128)}) %reduce-scatter.4.cloned.1.call-update) | async-done | bytes 524304 | tf_op jit(solution)/shard_map/reduce_scatter | solution.py:74
  389.6 5.6 copy.84
  395.2 300.0 %all-gather.8.cloned.1.call-done = f32[4096,256]{1,0:T(8,128)} async-done(((f32[32,256]{1,0:T(8,128)}), f32[4096,256]{1,0:T(8,128)}) %all-gather.8.cloned.1.call-update) | async-done | bytes 4194320 | tf_op jit(solution)/shard_map/all_gather | solution.py:78
  697.4 11.7 %cholesky.240 = f32[128,128]{1,0:T(8,128)S(1)} custom-call(f32[128,128]{1,0:T(8,128)S(1)} %cholesky.276), custom_call_target="Cholesky" | custom-call | tf_op jit(solution)/shard_map/jit(cholesky)/cholesky | solution.py:19
  709.7 9.8 %custom-call.19 = f32[1,128,128]{1,2,0:T(8,128)S(1)} custom-call(f32[1,128,128]{2,1,0:T(8,128)S(1)} %get-tuple-element.79), custom_call_target="InvertDiagBlocksLowerTriangular" | custom-call | tf_op jit(solution)/shard_map/jit(cholesky)/cholesky | solution.py:19
  720.1 11.7 %cholesky.257 = f32[128,128]{1,0:T(8,128)S(1)} custom-call(f32[128,128]{1,0:T(8,128)S(1)} %convolution_subtract_fusion.7), custom_call_target="Cholesky" | custom-call | tf_op jit(solution)/shard_map/jit(cholesky)/cholesky | solution.py:19
  734.1 4.1 while.8
  738.1 19.9 %custom-call.20 = f32[2,128,128]{1,2,0:T(8,128)S(1)} custom-call(f32[2,128,128]{2,1,0:T(8,128)S(1)} %get-tuple-element.27), custom_call_target="InvertDiagBlocksLowerTriangular" | custom-call | tf_op jit(solution)/shard_map/triangular_solve/custom-call.0 | solution.py:20
  758.0 3.7 fusion.7
  761.7 3.5 convolution_subtract_fusion.3
  765.3 2.0 fusion.23
  767.6 3.8 copy.96
  772.2 2.2 fusion.3
  (115 shorter events, 32.8 us)
Async XLA Ops:
  7.2 69.4 %all-gather.4.cloned.1.call-start = ((), (), s32[]{:S(2)}) async-start(), calls=%async_computation.2 | async-start | bytes 4456448 | tf_op jit(solution)/shard_map/all_gather | solution.py:45
  13.6 137.8 %all-gather.6.cloned.1.call-start = ((), (), s32[]{:S(2)}) async-start(), calls=%async_computation.3 | async-start | bytes 4456448 | tf_op jit(solution)/shard_map/all_gather | solution.py:46
  14.4 373.2 %reduce-scatter.4.cloned.1.call-start = ((), (), s32[]{:S(2)}) async-start(), calls=%async_computation.5 | async-start | bytes 4718592 | tf_op jit(solution)/shard_map/reduce_scatter | solution.py:74
  16.6 8.2 %copy-start.7 = (s32[1,16]{1,0:T(1,128)S(1)}, s32[1,16]{1,0:T(1,128)}, u32[]{:S(2)}) copy-start(s32[1,16]{1,0:T(1,128)} %param.13) | copy-start | bytes 196
  138.8 3.9 copy-start.4
  157.2 2.0 copy-start.1
  221.1 3.7 copy-start.2
  229.2 3.9 copy-start
  229.2 3.9 copy-start.3
  335.7 0.7 copy-start.8
  335.7 51.9 %copy-start.6 = (f32[4096,1,32]{0,2,1:T(8,128)S(1)}, f32[4096,1,32]{0,2,1:T(8,128)}, u32[]{:S(2)}) copy-start(f32[4096,1,32]{0,2,1:T(8,128)} %param.11) | copy-start | bytes 1572868
  335.7 359.5 %all-gather.8.cloned.1.call-start = ((), (), s32[]{:S(2)}) async-start(), calls=%async_computation.4 | async-start | bytes 4227072 | tf_op jit(solution)/shard_map/all_gather | solution.py:78
  758.0 3.7 copy-start.5
Sparse Core Ops, SparseCore 0:
  13.8 62.7 all-gather.3
  79.4 58.3 all-gather.5
  335.9 51.7 reduce-scatter.3
  389.7 305.4 all-gather.7
where the time goes:
time: 792 us; the launch traced here: 781 us
  waiting for transfers between devices  403 us (51%)
  other arithmetic  187 us (24%)
  local copies, waits for them, and re-layouts  72.4 us (9%)
  blocking collectives  54.1 us (7%)
  matrix products  40.5 us (5%)
  between operations  24.1 us (3%)
    all_gather x1, waiting for transfers between devices, shards(): raw_root = lax.all_gather(row, ('front', 'leaf'), axis=0, tiled=True)  300 us
    another operation x20, other arithmetic, make_panel(): lower = jnp.linalg.cholesky(diag_block)  103 us
    another operation x7, other arithmetic, make_panel(): lax.linalg.triangular_solve(lower, raw_column, left_side=False, lower=Tru...  60.1 us
    all_to_all x1, blocking collectives, shards(): lax.all_to_all(outgoing, 'front', split_axis=0, concat_axis=0, tiled=True)  54.1 us
    all_gather x1, waiting for transfers between devices, shards(): lax.all_gather(block_row(tiles, first).T, 'front', axis=0, tiled=True)  51.5 us
    reduce_scatter x1, waiting for transfers between devices, shards(): part = lax.psum_scatter(gathered, 'leaf', scatter_dimension=0, tiled=True)  51.2 us
    unnamed x25, local copies, waits for them, and re-layouts  31.1 us
    another operation x9, matrix products, make_panel(): lax.linalg.triangular_solve(lower, raw_column, left_side=False, lower=Tru...  22.8 us
  transfers between devices with their start and end apart: 4, of which 3 were waited for; matrix products, arithmetic and copies ran while one was open for 11% of the time, Pallas kernels for 0%

commit v1 on v0

--- a/solution.py
+++ b/solution.py
@@ -75,7 +75,12 @@
     part = part + root_front[:, 0, :].T
     pivot = root_order[0]
     row = lax.dynamic_slice_in_dim(part, pivot * block_size, block_size, 1)
-    raw_root = lax.all_gather(row, ("front", "leaf"), axis=0, tiled=True)
+    raw_root = jnp.concatenate(
+        lax.all_to_all(
+            jnp.stack([row] * lax.axis_size(("front", "leaf"))), ("front", "leaf"), 0, 0
+        ),
+        axis=0,
+    )
     panel = make_panel(raw_root, pivot, everything)
     own = lax.dynamic_slice_in_dim(panel, own_start + leaf_index * slice_width, slice_width, 0)
     part = part - jnp.dot(own, panel.T, precision=HIGH)

time: 792 us -> 540 us (0.68)
  waiting for transfers between devices: 403 us -> 149 us
    all_gather x1 -> x0, waiting for transfers between devices: 300 us -> none  [shards(): raw_root = lax.all_gather(row, ('front', 'leaf'), axis=0, tiled=True)]
    all_to_all x0 -> x1, waiting for transfers between devices: none -> 46.2 us  [shards(): lax.all_to_all(jnp.stack([row] * lax.axis_size(('front', 'leaf'))), ('fro...]
    unnamed x25 -> x22, local copies, waits for them, and re-layouts: 31.1 us -> 25.5 us
  transfers between devices with their start and end apart: 4 -> 4, of which waited for: 3 -> 3; matrix products, arithmetic and copies ran while one was open for 11% -> 17% of each run, Pallas kernels for 0% -> 0%
where the time goes in v1:
time: 540 us; the launch traced here: 529 us
  other arithmetic  185 us (34%)
  waiting for transfers between devices  149 us (28%)
  local copies, waits for them, and re-layouts  66 us (12%)
  blocking collectives  54.1 us (10%)
  matrix products  42.2 us (8%)
  between operations  25.2 us (5%)
  starting transfers between devices  7.84 us (1%)
    another operation x20, other arithmetic, make_panel(): lower = jnp.linalg.cholesky(diag_block)  103 us
    another operation x7, other arithmetic, make_panel(): lax.linalg.triangular_solve(lower, raw_column, left_side=False, lower=Tru...  59.9 us
    all_to_all x1, blocking collectives, shards(): lax.all_to_all(outgoing, 'front', split_axis=0, concat_axis=0, tiled=True)  54.1 us
    reduce_scatter x1, waiting for transfers between devices, shards(): part = lax.psum_scatter(gathered, 'leaf', scatter_dimension=0, tiled=True)  51.2 us
    all_gather x1, waiting for transfers between devices, shards(): lax.all_gather(block_row(tiles, first).T, 'front', axis=0, tiled=True)  50.6 us
    all_to_all x1, waiting for transfers between devices, shards(): lax.all_to_all(jnp.stack([row] * lax.axis_size(('front', 'leaf'))), ('fro...  46.2 us
    unnamed x22, local copies, waits for them, and re-layouts  25.5 us
    another operation x9, matrix products, make_panel(): lax.linalg.triangular_solve(lower, raw_column, left_side=False, lower=Tru...  24.3 us
  transfers between devices with their start and end apart: 4, of which 3 were waited for; matrix products, arithmetic and copies ran while one was open for 17% of the time, Pallas kernels for 0%

profile of v1, /device:TPU:1, one launch (start us, length us, event | category | flops | bytes accessed | tf_op | source)
XLA Modules:
  0.0 529.0 jit_solution(10848821269463079468)
XLA Ops:
  17.8 5.6 %copy.40 = f32[4096,256]{0,1:T(8,128)} copy(f32[4096,256]{1,0:T(8,128)} %param.10) | data formatting | bytes 8388608 | tf_op args[0]
  26.6 50.6 %all-gather.3.cloned.1.call-done = f32[4096,256]{0,1:T(8,128)} async-done(((f32[256,256]{0,1:T(8,128)}), f32[4096,256]{0,1:T(8,128)}) %all-gather.3.cloned.1.call-update) | async-done | bytes 4194320 | tf_op jit(solution)/shard_map/all_gather | solution.py:45
  79.4 11.7 %cholesky.172 = f32[128,128]{1,0:T(8,128)S(1)} custom-call(f32[128,128]{1,0:T(8,128)S(1)} %cholesky.270), custom_call_target="Cholesky" | custom-call | tf_op jit(solution)/shard_map/jit(cholesky)/cholesky | solution.py:19
  91.1 9.8 %custom-call.15 = f32[1,128,128]{1,2,0:T(8,128)S(1)} custom-call(f32[1,128,128]{2,1,0:T(8,128)S(1)} %get-tuple-element.83), custom_call_target="InvertDiagBlocksLowerTriangular" | custom-call | tf_op jit(solution)/shard_map/jit(cholesky)/cholesky | solution.py:19
  101.4 11.7 %cholesky.189 = f32[128,128]{1,0:T(8,128)S(1)} custom-call(f32[128,128]{1,0:T(8,128)S(1)} %convolution_subtract_fusion.9), custom_call_target="Cholesky" | custom-call | tf_op jit(solution)/shard_map/jit(cholesky)/cholesky | solution.py:19
  115.5 4.1 while.6
  119.6 20.0 %custom-call.16 = f32[2,128,128]{1,2,0:T(8,128)S(1)} custom-call(f32[2,128,128]{2,1,0:T(8,128)S(1)} %get-tuple-element.25), custom_call_target="InvertDiagBlocksLowerTriangular" | custom-call | tf_op jit(solution)/shard_map/triangular_solve/custom-call.0 | solution.py:20
  140.0 3.9 copy.57
  143.8 1.9 fusion.11
  145.8 2.1 convolution_subtract_fusion.5
  147.8 2.0 fusion.31
  149.8 2.8 fusion.4
  152.7 5.7 %convolution_subtract_fusion.2 = f32[4096,256]{0,1:T(8,128)S(1)} fusion(f32[4096,256]{0,1:T(8,128)} %all-gather.5.cloned.1.call-done, f32[4096,256]{0,1:T(8,128)} %fusion.4, s32[]{:T(128)S(6)} %select_n.119), kind=kOutput, calls=%fused_computation.10 | convolution fusion | flops 1611661312 | bytes 12845060 | tf_op jit(solution)/shard_map/dot_general | solution.py:51
  158.4 2.0 copy-done.1
  161.5 11.7 %cholesky.206 = f32[128,128]{1,0:T(8,128)S(1)} custom-call(f32[128,128]{1,0:T(8,128)S(1)} %cholesky.273), custom_call_target="Cholesky" | custom-call | tf_op jit(solution)/shard_map/jit(cholesky)/cholesky | solution.py:19
  173.9 9.8 %custom-call.17 = f32[1,128,128]{1,2,0:T(8,128)S(1)} custom-call(f32[1,128,128]{2,1,0:T(8,128)S(1)} %get-tuple-element.79), custom_call_target="InvertDiagBlocksLowerTriangular" | custom-call | tf_op jit(solution)/shard_map/jit(cholesky)/cholesky | solution.py:19
  184.2 11.7 %cholesky.223 = f32[128,128]{1,0:T(8,128)S(1)} custom-call(f32[128,128]{1,0:T(8,128)S(1)} %convolution_subtract_fusion.8), custom_call_target="Cholesky" | custom-call | tf_op jit(solution)/shard_map/jit(cholesky)/cholesky | solution.py:19
  198.1 4.0 while.7
  202.0 19.9 %custom-call.18 = f32[2,128,128]{1,2,0:T(8,128)S(1)} custom-call(f32[2,128,128]{2,1,0:T(8,128)S(1)} %get-tuple-element.26), custom_call_target="InvertDiagBlocksLowerTriangular" | custom-call | tf_op jit(solution)/shard_map/triangular_solve/custom-call.0 | solution.py:20
  221.9 3.6 fusion.9
  225.6 2.0 convolution_subtract_fusion.4
  227.6 2.0 fusion.27
  230.0 3.9 copy.58
  233.9 2.4 convolution_subtract_fusion.1
  237.2 6.2 %select_select_fusion.1 = (f32[4096,256]{0,1:T(8,128)}, f32[4096,256]{0,1:T(8,128)}) fusion(f32[4096,256]{0,1:T(8,128)S(1)} %copy-done, f32[4096,256]{0,1:T(8,128)S(1)} %fusion.5, pred[4096]{0:T(1024)(128)(4,1)S(1)} %broadcast_in_dim.165, pred[]{:T(512)S(6)} %eq.57, pred[]{:T(512)S(6)} %eq.54, f32[4096,256]{0,1:T(8,128)S(1)} %convolution_subtract_fusion.1, ...), kind=kOutput, calls=%fused_computation.27 | convolution fusion | flops 1614807040 | bytes 25432070 | tf_op jit(solution)/shard_map/dot_general | solution.py:59
  243.3 5.6 %copy.54 = f32[4096,256]{1,0:T(8,128)} copy(f32[4096,256]{0,1:T(8,128)} %get-tuple-element.91) | data formatting | bytes 8388608 | tf_op jit(solution)/shard_map/reshape | solution.py:61
  248.9 5.4 %select_select_fusion = f32[16,256,256]{2,1,0:T(8,128)} fusion(f32[16,256,256]{2,1,0:T(8,128)} %bitcast.149, pred[16]{0:T(512)(128)(4,1)S(1)} %get-tuple-element.94, pred[]{:T(512)} %bitcast.21), kind=kLoop, calls=%fused_computation.26 | loop fusion | flops 2097152 | bytes 8388625 | tf_op jit(solution)/shard_map/jit(_where)/select_n | solution.py:70
  254.3 4.9 gather_fusion
  259.3 2.8 broadcast_select_fusion
  262.1 54.1 %all_to_all.10 = f32[16,256,256]{2,1,0:T(8,128)} all-to-all(f32[16,256,256]{2,1,0:T(8,128)S(1)} %broadcast_select_fusion), channel_id=1, replica_groups=mesh['leaf'=8,'front'=16] {'front'}, dimensions={0} | all-to-all | bytes 8388608 | tf_op jit(solution)/shard_map/all_to_all | solution.py:71
  316.2 5.0 gather_fusion.1
  321.2 2.8 select_bitcast_fusion
  324.0 2.6 copy.56
  327.3 51.2 %reduce-scatter.2.cloned.1.call-done = f32[32,4096]{1,0:T(8,128)} async-done(((f32[256,4096]{1,0:T(8,128)}), f32[32,4096]{1,0:T(8,128)}) %reduce-scatter.2.cloned.1.call-update) | async-done | bytes 524304 | tf_op jit(solution)/shard_map/reduce_scatter | solution.py:74
  379.6 2.5 stack.2
  382.1 7.7 %all-to-all-start.1 = ((f32[128,32,256]{2,1,0:T(8,128)}), f32[128,32,256]{2,1,0:T(8,128)}, u32[]{:S(2)}, u32[]{:S(2)}) async-start(f32[128,32,256]{2,1,0:T(8,128)} %stack.2), calls=%async_computation.2 | async-start | bytes 8388608 | tf_op jit(solution)/shard_map/all_to_all | solution.py:79
  390.1 5.6 %copy.48 = f32[4096,256]{1,0:T(8,128)} copy(f32[4096,256]{0,1:T(8,128)} %get-tuple-element.90) | data formatting | bytes 8388608
  395.7 46.2 %all-to-all-done.1 = f32[128,32,256]{2,1,0:T(8,128)} async-done(((f32[128,32,256]{2,1,0:T(8,128)}), f32[128,32,256]{2,1,0:T(8,128)}, u32[]{:S(2)}, u32[]{:S(2)}) %all-to-all-start.1) | async-done | bytes 4194336 | tf_op jit(solution)/shard_map/all_to_all | solution.py:79
  444.0 11.7 %cholesky.240 = f32[128,128]{1,0:T(8,128)S(1)} custom-call(f32[128,128]{1,0:T(8,128)S(1)} %cholesky.276), custom_call_target="Cholesky" | custom-call | tf_op jit(solution)/shard_map/jit(cholesky)/cholesky | solution.py:19
  456.4 9.8 %custom-call.19 = f32[1,128,128]{1,2,0:T(8,128)S(1)} custom-call(f32[1,128,128]{2,1,0:T(8,128)S(1)} %get-tuple-element.75), custom_call_target="InvertDiagBlocksLowerTriangular" | custom-call | tf_op jit(solution)/shard_map/jit(cholesky)/cholesky | solution.py:19
  466.7 11.7 %cholesky.257 = f32[128,128]{1,0:T(8,128)S(1)} custom-call(f32[128,128]{1,0:T(8,128)S(1)} %convolution_subtract_fusion.7), custom_call_target="Cholesky" | custom-call | tf_op jit(solution)/shard_map/jit(cholesky)/cholesky | solution.py:19
  480.5 3.8 while.8
  484.3 19.9 %custom-call.20 = f32[2,128,128]{1,2,0:T(8,128)S(1)} custom-call(f32[2,128,128]{2,1,0:T(8,128)S(1)} %get-tuple-element.27), custom_call_target="InvertDiagBlocksLowerTriangular" | custom-call | tf_op jit(solution)/shard_map/triangular_solve/custom-call.0 | solution.py:20
  504.2 3.5 fusion.7
  507.7 5.1 convolution_subtract_fusion.3
  512.9 2.0 fusion.23
  515.3 3.8 copy.59
  519.9 2.2 fusion.3
  (112 shorter events, 34.4 us)
Async XLA Ops:
  7.2 70.1 %all-gather.3.cloned.1.call-start = ((), (), s32[]{:S(2)}) async-start(), calls=%async_computation.3 | async-start | bytes 4456448 | tf_op jit(solution)/shard_map/all_gather | solution.py:45
  14.4 138.3 %all-gather.5.cloned.1.call-start = ((), (), s32[]{:S(2)}) async-start(), calls=%async_computation.4 | async-start | bytes 4456448 | tf_op jit(solution)/shard_map/all_gather | solution.py:46
  15.1 363.4 %reduce-scatter.2.cloned.1.call-start = ((), (), s32[]{:S(2)}) async-start(), calls=%async_computation.5 | async-start | bytes 4718592 | tf_op jit(solution)/shard_map/reduce_scatter | solution.py:74
  17.8 8.7 %copy-start.6 = (s32[1,16]{1,0:T(1,128)S(1)}, s32[1,16]{1,0:T(1,128)}, u32[]{:S(2)}) copy-start(s32[1,16]{1,0:T(1,128)} %param.13) | copy-start | bytes 196
  140.0 3.9 copy-start.4
  158.3 2.0 copy-start.1
  221.9 3.7 copy-start.2
  230.0 3.9 copy-start
  230.0 3.9 copy-start.3
  326.6 0.7 copy-start.7
  326.6 51.9 %copy-start.5 = (f32[4096,1,32]{0,2,1:T(8,128)S(1)}, f32[4096,1,32]{0,2,1:T(8,128)}, u32[]{:S(2)}) copy-start(f32[4096,1,32]{0,2,1:T(8,128)} %param.11) | copy-start | bytes 1572868
  382.1 59.8 %all-to-all-start.1 = ((f32[128,32,256]{2,1,0:T(8,128)}), f32[128,32,256]{2,1,0:T(8,128)}, u32[]{:S(2)}, u32[]{:S(2)}) async-start(f32[128,32,256]{2,1,0:T(8,128)} %stack.2), calls=%async_computation.2 | async-start | bytes 8388608 | tf_op jit(solution)/shard_map/all_to_all | solution.py:79
Sparse Core Ops, SparseCore 0:
  14.5 62.7 all-gather.2
  80.1 58.1 all-gather.4
  326.8 51.6 reduce-scatter.1
